TPU v7x, 512 devices: a whole 4x8x8 slice. The times are simulated.
512 devices in a mesh: row: 32 (over z, y_hi, core), col: 16 (over x, y_lo).
Axes of the slice: x: 4, y: 8 (y_hi: 2, y_lo: 4; y = y_hi * 4 + y_lo), z: 8, core: 2. Of those that a mesh axis runs over, the one named last changes fastest.
Arguments:
- rhs_top: bfloat16 [2, 1024, 16384], P(None, 'row', 'col'), may hold values from -6 to 6
- diag_inverse: bfloat16 [2, 1024, 1024], P(None, 'row'), as said below
- panel_coupling: bfloat16 [1024, 1024], P('row'), may hold values from -0.1875 to 0.1875
- trailing_factor: bfloat16 [32768, 2048], P('row', 'col'), may hold values from -0.125 to 0.125
- rhs_trailing: bfloat16 [32768, 16384], P('row', 'col'), may hold values from -6 to 6
Outputs:
- solved: bfloat16 [2, 1024, 16384], P(None, 'row', 'col')
- updated: bfloat16 [32768, 16384], P('row', 'col')
Inputs may be any that keep to these rules, and one draw needn't show every extreme that they name: Each diag_inverse[k] is lower triangular.
All inputs are finite; a program needn't handle non-finite values.
Results may differ from a plain program's by a relative error of at most 0.0055.
Values may be sent and summed in bfloat16 or wider, within the bound.
A program may use at most 64 MiB of HBM per device.

v0:
```python
import jax
import jax.numpy as jnp
from jax import lax
from jax.sharding import PartitionSpec as P


def fold_rows(inverse_rows, piece):
    return jnp.dot(inverse_rows, piece, preferred_element_type=jnp.float32)


def shards(rhs_top, diag_inverse, panel_coupling, trailing_factor, rhs_trailing):
    inverse_first = diag_inverse[0]
    inverse_second = diag_inverse[1]
    first_mine = fold_rows(
        inverse_first, lax.all_gather(rhs_top[0], "row", axis=0, tiled=True)
    ).astype(jnp.bfloat16)
    first_all = lax.all_gather(first_mine, "row", axis=0, tiled=True)
    carried = (
        rhs_top[1].astype(jnp.float32)
        - jnp.dot(panel_coupling, first_all, preferred_element_type=jnp.float32)
    ).astype(jnp.bfloat16)
    second_mine = fold_rows(
        inverse_second, lax.all_gather(carried, "row", axis=0, tiled=True)
    ).astype(jnp.bfloat16)
    second_all = lax.all_gather(second_mine, "row", axis=0, tiled=True)
    solution = jnp.concatenate([first_all, second_all], axis=0)
    total = jnp.dot(
        lax.all_gather(trailing_factor, "col", axis=1, tiled=True),
        solution,
        preferred_element_type=jnp.float32,
    )
    updated = (rhs_trailing.astype(jnp.float32) - total).astype(jnp.bfloat16)
    solved = jnp.stack([first_mine, second_mine])
    return (solved, updated)


def solution(mesh):
    in_specs = (
        P(None, "row", "col"),
        P(None, "row", None),
        P("row", None),
        P("row", "col"),
        P("row", "col"),
    )
    out_specs = (P(None, "row", "col"), P("row", "col"))
    return jax.shard_map(shards, mesh=mesh, in_specs=in_specs, out_specs=out_specs, check_vma=False)
```

profile of v0, /device:TPU:1, one launch (start us, length us, event | category | flops | bytes accessed | tf_op | source)
XLA Modules:
  0.0 512.4 jit_solution(12273619999213910419)
XLA Ops:
  7.2 0.0 copy-start
  7.2 0.0 copy-start.5
  7.2 0.0 all-gather.15.cloned.1.call-start
  7.2 1.5 slice.13
  8.7 0.0 all-gather.15.cloned.1.call-update
  8.8 0.0 copy-start.4
  8.8 0.0 all-gather.7.cloned.1.call-start
  8.8 99.5 %all-gather.15.cloned.1.call-done = bf16[1,1024,1024]{2,1,0:T(8,128)(2,1)} async-done(((bf16[1,32,1024]{2,1,0:T(8,128)(2,1)}), bf16[1,1024,1024]{2,1,0:T(8,128)(2,1)}) %all-gather.15.cloned.1.call-update) | async-done | bytes 2097168 | tf_op jit(solution)/shard_map/all_gather | solution.py:15
  108.3 2.7 fusion.11
  111.0 0.0 all-gather.7.cloned.1.call-update
  111.0 0.0 copy-start.1
  111.1 0.0 all-gather.9.cloned.1.call-start
  111.1 88.3 %all-gather.7.cloned.1.call-done = bf16[1024,1024]{1,0:T(8,128)(2,1)} async-done(((bf16[32,1024]{1,0:T(8,128)(2,1)}), bf16[1024,1024]{1,0:T(8,128)(2,1)}) %all-gather.7.cloned.1.call-update) | async-done | bytes 2097168 | tf_op jit(solution)/shard_map/all_gather | solution.py:17
  199.4 0.0 copy-done
  199.4 0.0 copy-done.5
  199.4 2.7 fusion.10
  202.1 0.0 all-gather.9.cloned.1.call-update
  202.2 0.0 all-gather.13.cloned.1.call-start
  202.2 0.5 all-gather.13.cloned.1.call-update
  202.7 0.0 all-gather.11.cloned.1.call-start
  202.8 87.8 %all-gather.9.cloned.1.call-done = bf16[1024,1024]{1,0:T(8,128)(2,1)} async-done(((bf16[32,1024]{1,0:T(8,128)(2,1)}), bf16[1024,1024]{1,0:T(8,128)(2,1)}) %all-gather.9.cloned.1.call-update) | async-done | bytes 2097168 | tf_op jit(solution)/shard_map/all_gather | solution.py:23
  290.6 0.0 copy-done.4
  290.6 2.7 convolution_convert_fusion
  293.3 0.0 all-gather.11.cloned.1.call-update
  293.3 0.0 copy-done.1
  293.3 0.0 copy-start.2
  293.3 0.0 copy-start.3
  293.3 2.6 copy.7
  295.9 0.0 copy-done.2
  295.9 0.0 copy-done.3
  295.9 0.7 pad_maximum_fusion
  296.6 102.9 %all-gather.13.cloned.1.call-done = bf16[1024,2048]{1,0:T(8,128)(2,1)} async-done(((bf16[1024,128]{1,0:T(8,128)(2,1)}), bf16[1024,2048]{1,0:T(8,128)(2,1)}) %all-gather.13.cloned.1.call-update) | async-done | bytes 4194320 | tf_op jit(solution)/shard_map/all_gather | solution.py:28
  399.5 95.2 %all-gather.11.cloned.1.call-done = bf16[1024,1024]{1,0:T(8,128)(2,1)} async-done(((bf16[32,1024]{1,0:T(8,128)(2,1)}), bf16[1024,1024]{1,0:T(8,128)(2,1)}) %all-gather.11.cloned.1.call-update) | async-done | bytes 2097168 | tf_op jit(solution)/shard_map/all_gather | solution.py:25
  494.7 8.6 %fusion.4 = bf16[1024,1024]{0,1:T(8,128)(2,1)S(1)} fusion(bf16[1024,1024]{0,1:T(8,128)(2,1)} %copy.7, bf16[1024,2048]{1,0:T(8,128)(2,1)} %all-gather.13.cloned.1.call-done, bf16[1024,1024]{1,0:T(8,128)(2,1)} %all-gather.11.cloned.1.call-done, bf16[1024,1024]{1,0:T(8,128)(2,1)} %all-gather.7.cloned.1.call-done), kind=kOutput, calls=%fused_computation.5 | convolution fusion | flops 4306501632 | bytes 12582912 | tf_op jit(solution)/shard_map/dot_general | solution.py:27
  503.3 2.6 copy.8
Async XLA Ops:
  7.2 192.3 %copy-start = (bf16[32,1024]{1,0:T(8,128)(2,1)S(1)}, bf16[32,1024]{1,0:T(8,128)(2,1)}, u32[]{:S(2)}) copy-start(bf16[32,1024]{1,0:T(8,128)(2,1)} %param.7) | copy-start | bytes 196612
  7.2 192.3 %copy-start.5 = (bf16[2,32,1024]{2,1,0:T(8,128)(2,1)S(1)}, bf16[2,32,1024]{2,1,0:T(8,128)(2,1)}, u32[]{:S(2)}) copy-start(bf16[2,32,1024]{2,1,0:T(8,128)(2,1)} %param.5) | copy-start | bytes 393220
  7.2 101.1 %all-gather.15.cloned.1.call-start = ((), (), s32[]{:S(2)}) async-start(), calls=%async_computation.4 | async-start | bytes 2162688 | tf_op jit(solution)/shard_map/all_gather | solution.py:15
  8.8 281.8 %copy-start.4 = (bf16[2,32,1024]{2,1,0:T(8,128)(2,1)S(1)}, bf16[2,32,1024]{2,1,0:T(8,128)(2,1)}, u32[]{:S(2)}) copy-start(bf16[2,32,1024]{2,1,0:T(8,128)(2,1)} %param.6) | copy-start | bytes 393220
  8.8 190.7 %all-gather.7.cloned.1.call-start = ((), (), s32[]{:S(2)}) async-start(), calls=%async_computation | async-start | bytes 2162688 | tf_op jit(solution)/shard_map/all_gather | solution.py:17
  111.0 182.3 %copy-start.1 = (bf16[1024,1024]{1,0:T(8,128)(2,1)S(1)}, bf16[1024,1024]{1,0:T(8,128)(2,1)}, u32[]{:S(2)}) copy-start(bf16[1024,1024]{1,0:T(8,128)(2,1)} %param.9) | copy-start | bytes 6291460
  111.1 179.6 %all-gather.9.cloned.1.call-start = ((), (), s32[]{:S(2)}) async-start(), calls=%async_computation.1 | async-start | bytes 2162688 | tf_op jit(solution)/shard_map/all_gather | solution.py:23
  202.2 197.3 %all-gather.13.cloned.1.call-start = ((), (), s32[]{:S(2)}) async-start(), calls=%async_computation.3 | async-start | bytes 4456448 | tf_op jit(solution)/shard_map/all_gather | solution.py:28
  202.7 292.0 %all-gather.11.cloned.1.call-start = ((), (), s32[]{:S(2)}) async-start(), calls=%async_computation.2 | async-start | bytes 2162688 | tf_op jit(solution)/shard_map/all_gather | solution.py:25
  293.3 2.6 copy-start.2
  293.3 2.6 copy-start.3
Sparse Core Ops, SparseCore 0:
  12.0 96.2 all-gather.14
  112.2 87.1 all-gather.6
  203.4 87.1 all-gather.8
  292.5 106.9 all-gather.12
  402.7 91.9 all-gather.10
where the time goes:
time: 514 us; the launch traced here: 512 us
  waiting for transfers between devices  474 us (92%)
  matrix products  16.7 us (3%)
  between operations  13.8 us (3%)
  local copies, waits for them, and re-layouts  6.67 us (1%)
    all_gather x1, waiting for transfers between devices, shards(): lax.all_gather(trailing_factor, 'col', axis=1, tiled=True)  103 us
    all_gather x1, waiting for transfers between devices, shards(): lax.all_gather(rhs_top[0], 'row', axis=0, tiled=True)  99.5 us
    all_gather x1, waiting for transfers between devices, shards(): second_all = lax.all_gather(second_mine, 'row', axis=0, tiled=True)  95.2 us
    all_gather x1, waiting for transfers between devices, shards(): first_all = lax.all_gather(first_mine, 'row', axis=0, tiled=True)  88.3 us
    all_gather x1, waiting for transfers between devices, shards(): lax.all_gather(carried, 'row', axis=0, tiled=True)  87.8 us
  transfers between devices with their start and end apart: 5, of which 5 were waited for; matrix products, arithmetic and copies ran while one was open for 1% of the time, Pallas kernels for 0%

commit v1 on v0

v1 whole, which is shorter than its diff:
```python
import jax
import jax.numpy as jnp
from jax import lax
from jax.experimental import pallas as pl
from jax.experimental.pallas import tpu as pltpu
from jax.sharding import PartitionSpec as P

MESH = pl.DeviceIdType.MESH
BF = jnp.bfloat16
F32 = jnp.float32

R0, D0, CP, R1, D1 = range(5)
STAGES = ((0, 2), (2, 4), (4, 5))


def kernel(
    rhs_ref, diag_ref, coup_ref, fac_ref, trail_ref,
    solved_ref, upd_ref,
    pan, sol, car, fac, trail, acc, out,
    recv, lrecv, send, lsend, local,
):
    row = lax.axis_index("row")
    col = lax.axis_index("col")
    z, yh, k = row // 4, (row // 2) % 2, row % 2
    x, yl = col // 4, col % 4
    mid = (yl // 2 + yl % 2) % 2 == 1
    sib = row + 1 - 2 * k
    zup, zdn = (row + 4) % 32, (row + 28) % 32
    mate = row + 2 - 4 * yh
    xup, xdn = (col + 4) % 16, (col + 12) % 16
    y1 = x * 4 + yl + 1 - 2 * (yl % 2)
    y2 = x * 4 + 3 - yl

    mine = pl.ds(pl.multiple_of(row * 32, 32), 32)
    loads = [
        pltpu.make_async_copy(rhs_ref.at[0], pan.at[R0, mine, :], local.at[0]),
        pltpu.make_async_copy(diag_ref.at[0], pan.at[D0, mine, :], local.at[1]),
        pltpu.make_async_copy(fac_ref, fac.at[col], local.at[2]),
        pltpu.make_async_copy(coup_ref, pan.at[CP, mine, :], local.at[3]),
        pltpu.make_async_copy(rhs_ref.at[1], pan.at[R1, mine, :], local.at[4]),
        pltpu.make_async_copy(diag_ref.at[1], pan.at[D1, mine, :], local.at[5]),
        pltpu.make_async_copy(trail_ref, trail, local.at[6]),
    ]
    for load in loads:
        load.start()

    barrier = pltpu.get_barrier_semaphore()
    peers = [(sib, col), (zup, col), (zdn, col), (mate, col), (row, xup), (row, xdn), (row, y1)]
    for peer in peers:
        pl.semaphore_signal(barrier, inc=1, device_id=peer, device_id_type=MESH)

    @pl.when(mid)
    def _():
        pl.semaphore_signal(barrier, inc=1, device_id=(row, y2), device_id_type=MESH)
        pl.semaphore_wait(barrier, len(peers) + 1)

    @pl.when(jnp.logical_not(mid))
    def _():
        pl.semaphore_wait(barrier, len(peers))

    sent = []
    later = []
    pushes = [0]

    def block(stage, q):
        low, high = STAGES[stage]
        return pan.at[low:high, pl.ds(pl.multiple_of(q * 32, 32), 32), :]

    def pcopy(stage, q, to, sem):
        return pltpu.make_async_remote_copy(
            src_ref=block(stage, q), dst_ref=block(stage, q),
            send_sem=sem, recv_sem=recv.at[stage, q],
            device_id=(to, col), device_id_type=MESH,
        )

    def push(stage, q, to):
        copy = pcopy(stage, q, to, send.at[pushes[0]])
        pushes[0] += 1
        copy.start()
        sent.append(copy)

    def arrive(stage, q):
        pcopy(stage, q, sib, send.at[0]).wait_recv()

    def rank(zz, j):
        return zz * 4 + (yh + j * (1 - 2 * yh)) * 2 + k

    def own(stage):
        for to in (zup, zdn, mate, sib):
            push(stage, row, to)

    def pair(stage):
        arrive(stage, mate)
        for to in (zup, zdn, sib):
            push(stage, mate, to)

    def hop(stage, h):
        for j in (0, 1):
            if h < 4 or j == 0:
                q = rank((z + 8 - h) % 8, j)
                arrive(stage, q)
                if h < 3 or (h == 3 and j == 0):
                    push(stage, q, zup)
                push(stage, q, sib)
            if h < 4 or j == 1:
                q = rank((z + h) % 8, j)
                arrive(stage, q)
                if h < 3 or (h == 3 and j == 1):
                    push(stage, q, zdn)
                push(stage, q, sib)

    def fill(stage):
        @pl.loop(0, 16)
        def _(i):
            arrive(stage, i * 2 + 1 - k)

    def lcopy(c, to, sem):
        return pltpu.make_async_remote_copy(
            src_ref=fac.at[c], dst_ref=fac.at[c],
            send_sem=sem, recv_sem=lrecv.at[c],
            device_id=(row, to), device_id_type=MESH,
        )

    count = [0]

    def lpush(c, to, wait=True):
        copy = lcopy(c, to, lsend.at[count[0]])
        copy.start()
        if wait:
            sent.append(copy)
        else:
            later.append((c, to, count[0]))
        count[0] += 1

    def larrive(c):
        lcopy(c, xup, lsend.at[0]).wait_recv()

    def lown():
        lpush(col, y1)

        @pl.when(mid)
        def _():
            lpush(col, y2, False)

        lpush(col, xup)
        lpush(col, xdn)

    order = [
        yl + 1 - 2 * (yl % 2),
        2 - yl // 2,
        3 - 3 * (yl // 2),
    ]

    def line(d):
        c = x * 4 + order[d]
        larrive(c)

        @pl.when(mid)
        def _():
            lpush(c, y2 if d == 0 else y1, False)

        lpush(c, xup)
        lpush(c, xdn)

    def ring(m):
        e = [yl, order[0], order[1], order[2]][m]
        below = (x + 3) % 4 * 4 + e
        above = (x + 1) % 4 * 4 + e
        larrive(below)
        if m % 2 == 0:
            lpush(below, xup)
        larrive(above)
        if m % 2 == 1:
            lpush(above, xdn)

    def ringlast():
        for e in (yl, order[0], order[1], order[2]):
            larrive((x + 2) % 4 * 4 + e)

    def first():
        @pl.loop(0, 4)
        def _(n):
            cols = pl.ds(pl.multiple_of(n * 256, 256), 256)
            for i in (0, 1):
                deep = 512 * (i + 1)
                sol[pl.ds(512 * i, 512), cols] = jnp.dot(
                    pan[D0, pl.ds(512 * i, 512), :deep], pan[R0, :deep, cols],
                    preferred_element_type=F32,
                ).astype(BF)

    def carried():
        @pl.loop(0, 4)
        def _(n):
            cols = pl.ds(pl.multiple_of(n * 256, 256), 256)
            for i in (0, 1):
                rows = pl.ds(512 * i, 512)
                car[rows, cols] = (
                    pan[R1, rows, cols].astype(F32)
                    - jnp.dot(pan[CP, rows, :], sol[:1024, cols], preferred_element_type=F32)
                ).astype(BF)

    def second():
        @pl.loop(0, 4)
        def _(n):
            cols = pl.ds(pl.multiple_of(n * 256, 256), 256)
            for i in (0, 1):
                deep = 512 * (i + 1)
                sol[pl.ds(1024 + 512 * i, 512), cols] = jnp.dot(
                    pan[D1, pl.ds(512 * i, 512), :deep], car[:deep, cols],
                    preferred_element_type=F32,
                ).astype(BF)

    def product(half, rows, cols):
        left = jnp.concatenate([fac[8 * half + b, rows, :] for b in range(8)], axis=1)
        return jnp.dot(left, sol[pl.ds(1024 * half, 1024), cols], preferred_element_type=F32)

    def update_first():
        @pl.loop(0, 4)
        def _(n):
            cols = pl.ds(pl.multiple_of(n * 256, 256), 256)
            for i in (0, 1):
                rows = pl.ds(512 * i, 512)
                acc[rows, cols] = trail[rows, cols].astype(F32) - product(0, rows, cols)

    def stored(n):
        cols = pl.ds(pl.multiple_of(n * 256, 256), 256)
        return pltpu.make_async_copy(out.at[:, cols], upd_ref.at[:, cols], local.at[9 + n])

    def update_second():
        @pl.loop(0, 4)
        def _(n):
            cols = pl.ds(pl.multiple_of(n * 256, 256), 256)
            for i in (0, 1):
                rows = pl.ds(512 * i, 512)
                out[rows, cols] = (acc[rows, cols] - product(1, rows, cols)).astype(BF)
            stored(n).start()

    loads[0].wait()
    loads[1].wait()
    own(0)
    loads[2].wait()
    lown()
    pair(0)
    line(0)
    hop(0, 1)
    loads[3].wait()
    loads[4].wait()
    loads[5].wait()
    own(1)
    line(1)
    hop(0, 2)
    line(2)
    pair(1)
    hop(0, 3)
    ring(0)
    hop(0, 4)
    hop(1, 1)
    own(2)
    fill(0)
    first()
    keep = [pltpu.make_async_copy(sol.at[mine, :], solved_ref.at[0], local.at[7])]
    keep[0].start()
    hop(1, 2)
    ring(1)
    pair(2)
    hop(1, 3)
    ring(2)
    hop(1, 4)
    hop(2, 1)
    fill(1)
    carried()
    hop(2, 2)
    ring(3)
    ringlast()
    hop(2, 3)
    loads[6].wait()
    update_first()
    hop(2, 4)
    fill(2)
    second()
    low = pl.ds(pl.multiple_of(1024 + row * 32, 32), 32)
    keep.append(pltpu.make_async_copy(sol.at[low, :], solved_ref.at[1], local.at[8]))
    keep[1].start()
    update_second()
    for copy in sent:
        copy.wait_send()

    @pl.when(mid)
    def _():
        for c, to, at in later:
            lcopy(c, to, lsend.at[at]).wait_send()

    for copy in keep:
        copy.wait()
    for n in range(4):
        stored(n).wait()


def shards(rhs_top, diag_inverse, panel_coupling, trailing_factor, rhs_trailing):
    anywhere = pl.BlockSpec(memory_space=pl.ANY)
    dma = pltpu.SemaphoreType.DMA
    return pl.pallas_call(
        kernel,
        out_shape=(
            jax.ShapeDtypeStruct((2, 32, 1024), BF),
            jax.ShapeDtypeStruct((1024, 1024), BF),
        ),
        in_specs=[anywhere] * 5,
        out_specs=(anywhere, anywhere),
        scratch_shapes=[
            pltpu.VMEM((5, 1024, 1024), BF),
            pltpu.VMEM((2048, 1024), BF),
            pltpu.VMEM((1024, 1024), BF),
            pltpu.VMEM((16, 1024, 128), BF),
            pltpu.VMEM((1024, 1024), BF),
            pltpu.VMEM((1024, 1024), F32),
            pltpu.VMEM((1024, 1024), BF),
            dma((3, 32)),
            dma((16,)),
            dma((93,)),
            dma((17,)),
            dma((13,)),
        ],
        compiler_params=pltpu.CompilerParams(
            collective_id=0, has_side_effects=True, vmem_limit_bytes=50 * 1024 * 1024
        ),
        name="substitute",
    )(rhs_top, diag_inverse, panel_coupling, trailing_factor, rhs_trailing)


def solution(mesh):
    in_specs = (
        P(None, "row", "col"),
        P(None, "row", None),
        P("row", None),
        P("row", "col"),
        P("row", "col"),
    )
    out_specs = (P(None, "row", "col"), P("row", "col"))
    return jax.shard_map(shards, mesh=mesh, in_specs=in_specs, out_specs=out_specs, check_vma=False)
```

time: 514 us -> 107 us (0.21)
  waiting for transfers between devices: 474 us -> 0 us
  Pallas kernels: 0 us -> 100 us
  matrix products: 16.7 us -> 0 us
  between operations: 13.8 us -> 0.65 us
    all_gather x5 -> x0, waiting for transfers between devices: 474 us -> none  [the longest x1 103 us: shards(): lax.all_gather(trailing_factor, 'col', axis=1, tiled=True)]
    pallas_call x0 -> x1, Pallas kernels: none -> 100 us  [shards(): pl.pallas_call(kernel, out_shape=(jax.ShapeDtypeStruct((2, 32, 1024), BF)...]
    dot_general x4 -> x0, matrix products: 16.7 us -> none  [the longest x1 8.59 us: shards(): jnp.dot(lax.all_gather(trailing_factor, 'col', axis=1, tiled=True), solut...]
  transfers between devices with their start and end apart: 5 -> 0, of which waited for: 5 -> 0; matrix products, arithmetic and copies ran while one was open for 1% -> 0% of each run, Pallas kernels for 0% -> 0%
where the time goes in v1:
time: 107 us; the launch traced here: 106 us
  Pallas kernels  100 us (93%)
  local copies, waits for them, and re-layouts  5.57 us (5%)
    pallas_call x1, Pallas kernels, shards(): pl.pallas_call(kernel, out_shape=(jax.ShapeDtypeStruct((2, 32, 1024), BF)...  100 us
    unnamed x10, local copies, waits for them, and re-layouts  5.57 us

profile of v1, /device:TPU:1, one launch (start us, length us, event | category | flops | bytes accessed | tf_op | source)
XLA Modules:
  0.0 106.4 jit_solution(799920837516212615)
XLA Ops:
  0.6 0.0 copy-start
  0.6 0.9 copy-done
  1.6 0.0 copy-start.1
  1.6 0.9 copy-done.1
  2.5 0.0 copy-start.2
  2.5 0.9 copy-done.2
  3.4 0.0 copy-start.3
  3.4 0.8 copy-done.3
  4.2 100.2 %substitute.1 = (bf16[2,32,1024]{2,1,0:T(8,128)(2,1)S(1)}, bf16[1024,1024]{1,0:T(8,128)(2,1)S(1)}) custom-call(bf16[2,32,1024]{2,1,0:T(8,128)(2,1)S(1)} %copy-done.1, bf16[2,32,1024]{2,1,0:T(8,128)(2,1)S(1)} %copy-done.2, bf16[32,1024]{1,0:T(8,128)(2,1)S(1)} %copy-done.3, bf16[1024,128]{1,0:T(8,128)(2,1)S(1)} %copy-done, bf16[1024,1024]{1,0:T(8,128)(2,1)} %trail_ref.1), custom_call_target="tpu_custom_call" | custom-call | tf_op jit(solution)/shard_map/substitute/pallas_call | solution.py:302
  104.4 0.7 copy.9
  105.1 1.3 %copy.10 = bf16[1024,1024]{1,0:T(8,128)(2,1)} copy(bf16[1024,1024]{1,0:T(8,128)(2,1)S(1)} %get-tuple-element.5) | data formatting | bytes 4194304
Async XLA Ops:
  0.6 1.0 copy-start
  1.6 0.9 copy-start.1
  2.5 0.9 copy-start.2
  3.4 0.8 copy-start.3

commit v2 on v0

v2 whole, which is shorter than its diff:
```python
import jax
import jax.numpy as jnp
from jax import lax
from jax.experimental import pallas as pl
from jax.experimental.pallas import tpu as pltpu
from jax.sharding import PartitionSpec as P

MESH = pl.DeviceIdType.MESH
BF = jnp.bfloat16
F32 = jnp.float32

RHS0, INV0, MID, INV1 = range(4)
STAGES = ((RHS0, INV0), (MID,), (INV1,))


def kernel(
    rhs_ref, diag_ref, coup_ref, fac_ref, trail_ref,
    solved_ref, upd_ref,
    pan, dia, sol, car, fac, trail, acc, out,
    recv, lrecv, send, lsend, local, kept, stores,
):
    row = lax.axis_index("row")
    col = lax.axis_index("col")
    z, yh, k = row // 4, (row // 2) % 2, row % 2
    x, yl = col // 4, col % 4
    mid = (yl // 2 + yl % 2) % 2 == 1
    sib = row + 1 - 2 * k
    zup, zdn = (row + 4) % 32, (row + 28) % 32
    mate = row + 2 - 4 * yh
    xup, xdn = (col + 4) % 16, (col + 12) % 16
    y1 = x * 4 + yl + 1 - 2 * (yl % 2)
    y2 = x * 4 + 3 - yl

    def rows_of(q):
        return pl.ds(pl.multiple_of(q * 32, 32), 32)

    mine = rows_of(row)

    def inverse_loads(p, at):
        return [
            pltpu.make_async_copy(
                diag_ref.at[p, :, pl.ds(256 * j, 256)], dia.at[p, j, mine, :], local.at[at + j]
            )
            for j in range(4)
        ]

    load_a = [pltpu.make_async_copy(rhs_ref.at[0], pan.at[0, mine, :], local.at[0])] + inverse_loads(0, 1)
    load_f = [pltpu.make_async_copy(fac_ref, fac.at[col], local.at[5])]
    load_b = [
        pltpu.make_async_copy(coup_ref, pan.at[1, mine, :], local.at[6]),
        pltpu.make_async_copy(rhs_ref.at[1], pan.at[2, mine, :], local.at[7]),
    ]
    load_c = inverse_loads(1, 8)
    load_t = [pltpu.make_async_copy(trail_ref, trail, local.at[12])]
    for load in load_a + load_f + load_b + load_c + load_t:
        load.start()

    def ready(loads):
        for load in loads:
            load.wait()

    barrier = pltpu.get_barrier_semaphore()
    peers = [(sib, col), (zup, col), (zdn, col), (mate, col), (row, xup), (row, xdn), (row, y1)]
    for peer in peers:
        pl.semaphore_signal(barrier, inc=1, device_id=peer, device_id_type=MESH)

    @pl.when(mid)
    def _():
        pl.semaphore_signal(barrier, inc=1, device_id=(row, y2), device_id_type=MESH)
        pl.semaphore_wait(barrier, len(peers) + 1)

    @pl.when(jnp.logical_not(mid))
    def _():
        pl.semaphore_wait(barrier, len(peers))

    def view(flow, q, chunks):
        if flow == RHS0:
            return pan.at[0, rows_of(q), :]
        if flow == MID:
            return pan.at[1:3, rows_of(q), :]
        return dia.at[0 if flow == INV0 else 1, 0:chunks, rows_of(q), :]

    def each_size(flow, q, act):
        if flow in (RHS0, MID):
            act(0)
        else:
            for chunks in (1, 2, 3, 4):

                @pl.when(q // 8 + 1 == chunks)
                def _(chunks=chunks):
                    act(chunks)

    def pcopy(flow, q, to, at, chunks):
        return pltpu.make_async_remote_copy(
            src_ref=view(flow, q, chunks), dst_ref=view(flow, q, chunks),
            send_sem=send.at[at], recv_sem=recv.at[flow, q],
            device_id=(to, col), device_id_type=MESH,
        )

    sent = []
    used = [0]

    def push(flow, q, targets):
        first_at = used[0]
        used[0] += len(targets)

        def act(chunks):
            for i, to in enumerate(targets):
                pcopy(flow, q, to, first_at + i, chunks).start()

        each_size(flow, q, act)
        sent.append((flow, q, targets, first_at))

    def arrive(flow, q):
        each_size(flow, q, lambda chunks: pcopy(flow, q, sib, 0, chunks).wait_recv())

    def own(stage):
        for flow in STAGES[stage]:
            push(flow, row, (zup, zdn, mate, sib))

    def pair(stage):
        for flow in STAGES[stage]:
            arrive(flow, mate)
            push(flow, mate, (zup, zdn, sib))

    def hop(stage, h, j):
        lane = (yh + j * (1 - 2 * yh)) * 2 + k
        for flow in STAGES[stage]:
            if h < 4 or j == 0:
                q = (z + 8 - h) % 8 * 4 + lane
                arrive(flow, q)
                push(flow, q, (zup, sib) if h < 3 or (h == 3 and j == 0) else (sib,))
            if h < 4 or j == 1:
                q = (z + h) % 8 * 4 + lane
                arrive(flow, q)
                push(flow, q, (zdn, sib) if h < 3 or (h == 3 and j == 1) else (sib,))

    def fill(stage):
        @pl.loop(0, 16)
        def _(i):
            for flow in STAGES[stage]:
                arrive(flow, i * 2 + 1 - k)

    def lcopy(c, to, at):
        return pltpu.make_async_remote_copy(
            src_ref=fac.at[c], dst_ref=fac.at[c],
            send_sem=lsend.at[at], recv_sem=lrecv.at[c],
            device_id=(row, to), device_id_type=MESH,
        )

    always, middle = [], []

    def lpush(c, to, record):
        at = len(always) + len(middle)
        lcopy(c, to, at).start()
        record.append((c, to, at))

    def larrive(c):
        lcopy(c, xup, 0).wait_recv()

    def spread(c, inner):
        @pl.when(mid)
        def _():
            lpush(c, inner, middle)

        lpush(c, xup, always)
        lpush(c, xdn, always)

    def lown():
        lpush(col, y1, always)
        spread(col, y2)

    order = [yl, yl + 1 - 2 * (yl % 2), 2 - yl // 2, 3 - 3 * (yl // 2)]

    def line(d):
        c = x * 4 + order[d]
        larrive(c)
        spread(c, y2 if d == 1 else y1)

    def ring(m):
        below = (x + 3) % 4 * 4 + order[m]
        above = (x + 1) % 4 * 4 + order[m]
        larrive(below)
        if m % 2 == 0:
            lpush(below, xup, always)
        larrive(above)
        if m % 2 == 1:
            lpush(above, xdn, always)

    def ringlast():
        for e in order:
            larrive((x + 2) % 4 * 4 + e)

    def lower(p, i, right):
        left = jnp.concatenate([dia[p, j, pl.ds(256 * i, 256), :] for j in range(i + 1)], axis=1)
        return jnp.dot(left, right, preferred_element_type=F32).astype(BF)

    def first(i):
        sol[pl.ds(256 * i, 256), :] = lower(0, i, pan[0, : 256 * (i + 1), :])

    def second(i):
        sol[pl.ds(1024 + 256 * i, 256), :] = lower(1, i, car[: 256 * (i + 1), :])

    def carried(low, high):
        @pl.loop(low, high)
        def _(i):
            rows = pl.ds(pl.multiple_of(i * 256, 256), 256)
            car[rows, :] = (
                pan[2, rows, :].astype(F32)
                - jnp.dot(pan[1, rows, :], sol[:1024, :], preferred_element_type=F32)
            ).astype(BF)

    def product(half, rows):
        left = jnp.concatenate([fac[8 * half + b, rows, :] for b in range(8)], axis=1)
        return jnp.dot(left, sol[pl.ds(1024 * half, 1024), :], preferred_element_type=F32)

    def update_first(low, high):
        @pl.loop(low, high)
        def _(i):
            rows = pl.ds(pl.multiple_of(i * 256, 256), 256)
            acc[rows, :] = trail[rows, :].astype(F32) - product(0, rows)

    def stored(i):
        rows = pl.ds(pl.multiple_of(i * 256, 256), 256)
        return pltpu.make_async_copy(out.at[rows, :], upd_ref.at[rows, :], stores.at[i])

    def update_second():
        @pl.loop(0, 4)
        def _(i):
            rows = pl.ds(pl.multiple_of(i * 256, 256), 256)
            out[rows, :] = (acc[rows, :] - product(1, rows)).astype(BF)
            stored(i).start()

    def keep(p):
        rows = pl.ds(pl.multiple_of(1024 * p + row * 32, 32), 32)
        return pltpu.make_async_copy(sol.at[rows, :], solved_ref.at[p], kept.at[p])

    ready(load_a)
    own(0)
    ready(load_f)
    lown()
    ready(load_b)
    own(1)
    ready(load_c)
    hop(0, 1, 0)
    pair(0)
    line(1)
    hop(0, 2, 0)
    ring(0)
    hop(0, 1, 1)
    hop(0, 3, 0)
    line(2)
    hop(0, 2, 1)
    hop(0, 4, 0)
    ring(1)
    pair(1)
    hop(1, 1, 0)
    own(2)
    hop(0, 3, 1)
    line(3)
    hop(1, 2, 0)
    hop(0, 4, 1)
    ring(2)
    hop(1, 1, 1)
    fill(0)
    first(0)
    first(1)
    hop(1, 3, 0)
    first(2)
    hop(1, 2, 1)
    first(3)
    keep(0).start()
    pair(2)
    hop(1, 4, 0)
    hop(2, 1, 0)
    ring(3)
    hop(1, 3, 1)
    hop(2, 2, 0)
    hop(1, 4, 1)
    hop(2, 1, 1)
    fill(1)
    carried(0, 2)
    hop(2, 3, 0)
    carried(2, 4)
    hop(2, 2, 1)
    hop(2, 4, 0)
    ringlast()
    ready(load_t)
    update_first(0, 2)
    hop(2, 3, 1)
    update_first(2, 4)
    hop(2, 4, 1)
    fill(2)
    for i in range(4):
        second(i)
    keep(1).start()
    update_second()

    for flow, q, targets, first_at in sent:

        def act(chunks, flow=flow, q=q, targets=targets, first_at=first_at):
            for i, to in enumerate(targets):
                pcopy(flow, q, to, first_at + i, chunks).wait_send()

        each_size(flow, q, act)
    for c, to, at in always:
        lcopy(c, to, at).wait_send()

    @pl.when(mid)
    def _():
        for c, to, at in middle:
            lcopy(c, to, at).wait_send()

    keep(0).wait()
    keep(1).wait()
    for i in range(4):
        stored(i).wait()


def shards(rhs_top, diag_inverse, panel_coupling, trailing_factor, rhs_trailing):
    anywhere = pl.BlockSpec(memory_space=pl.ANY)
    dma = pltpu.SemaphoreType.DMA
    return pl.pallas_call(
        kernel,
        out_shape=(
            jax.ShapeDtypeStruct((2, 32, 1024), BF),
            jax.ShapeDtypeStruct((1024, 1024), BF),
        ),
        in_specs=[anywhere] * 5,
        out_specs=(anywhere, anywhere),
        scratch_shapes=[
            pltpu.VMEM((3, 1024, 1024), BF),
            pltpu.VMEM((2, 4, 1024, 256), BF),
            pltpu.VMEM((2048, 1024), BF),
            pltpu.VMEM((1024, 1024), BF),
            pltpu.VMEM((16, 1024, 128), BF),
            pltpu.VMEM((1024, 1024), BF),
            pltpu.VMEM((1024, 1024), F32),
            pltpu.VMEM((1024, 1024), BF),
            dma((4, 32)),
            dma((16,)),
            dma((124,)),
            dma((17,)),
            dma((13,)),
            dma((2,)),
            dma((4,)),
        ],
        compiler_params=pltpu.CompilerParams(
            collective_id=0, has_side_effects=True, vmem_limit_bytes=60 * 1024 * 1024
        ),
        name="substitute",
    )(rhs_top, diag_inverse, panel_coupling, trailing_factor, rhs_trailing)


def solution(mesh):
    in_specs = (
        P(None, "row", "col"),
        P(None, "row", None),
        P("row", None),
        P("row", "col"),
        P("row", "col"),
    )
    out_specs = (P(None, "row", "col"), P("row", "col"))
    return jax.shard_map(shards, mesh=mesh, in_specs=in_specs, out_specs=out_specs, check_vma=False)
```

time: 514 us -> 93.6 us (0.18)
  waiting for transfers between devices: 474 us -> 0 us
  Pallas kernels: 0 us -> 88.2 us
  matrix products: 16.7 us -> 0 us
  between operations: 13.8 us -> 0.64 us
    all_gather x5 -> x0, waiting for transfers between devices: 474 us -> none  [the longest x1 103 us: shards(): lax.all_gather(trailing_factor, 'col', axis=1, tiled=True)]
    pallas_call x0 -> x1, Pallas kernels: none -> 88.2 us  [shards(): pl.pallas_call(kernel, out_shape=(jax.ShapeDtypeStruct((2, 32, 1024), BF)...]
    dot_general x4 -> x0, matrix products: 16.7 us -> none  [the longest x1 8.59 us: shards(): jnp.dot(lax.all_gather(trailing_factor, 'col', axis=1, tiled=True), solut...]
  transfers between devices with their start and end apart: 5 -> 0, of which waited for: 5 -> 0; matrix products, arithmetic and copies ran while one was open for 1% -> 0% of each run, Pallas kernels for 0% -> 0%
where the time goes in v2:
time: 93.6 us; the launch traced here: 93.5 us
  Pallas kernels  88.2 us (94%)
  local copies, waits for them, and re-layouts  4.65 us (5%)
    pallas_call x1, Pallas kernels, shards(): pl.pallas_call(kernel, out_shape=(jax.ShapeDtypeStruct((2, 32, 1024), BF)...  88.2 us
    unnamed x2, local copies, waits for them, and re-layouts  4.65 us

profile of v2, /device:TPU:1, one launch (start us, length us, event | category | flops | bytes accessed | tf_op | source)
XLA Modules:
  0.0 93.5 jit_solution(16012399249179322756)
XLA Ops:
  0.6 88.2 %substitute.1 = (bf16[2,32,1024]{2,1,0:T(8,128)(2,1)}, bf16[1024,1024]{1,0:T(8,128)(2,1)}) custom-call(bf16[2,32,1024]{2,1,0:T(8,128)(2,1)} %rhs_ref.1, bf16[2,32,1024]{2,1,0:T(8,128)(2,1)} %diag_ref.1, bf16[32,1024]{1,0:T(8,128)(2,1)} %coup_ref.1, bf16[1024,128]{1,0:T(8,128)(2,1)} %fac_ref.1, bf16[1024,1024]{1,0:T(8,128)(2,1)} %trail_ref.1), custom_call_target="tpu_custom_call" | custom-call | tf_op jit(solution)/shard_map/substitute/pallas_call | solution.py:323
  88.8 1.6 %copy.9 = bf16[2,32,1024]{2,1,0:T(8,128)(2,1)} copy(bf16[2,32,1024]{2,1,0:T(8,128)(2,1)} %get-tuple-element.4) | data formatting | bytes 262144
  90.4 3.1 %copy.10 = bf16[1024,1024]{1,0:T(8,128)(2,1)} copy(bf16[1024,1024]{1,0:T(8,128)(2,1)} %get-tuple-element.5) | data formatting | bytes 4194304

commit v3 on v2

--- a/solution.py
+++ b/solution.py
@@ -244,55 +244,56 @@
     ready(load_c)
     hop(0, 1, 0)
     pair(0)
+    hop(0, 2, 0)
+    hop(1, 1, 0)
     line(1)
-    hop(0, 2, 0)
     ring(0)
+    own(2)
     hop(0, 1, 1)
+    pair(1)
     hop(0, 3, 0)
+    hop(1, 2, 0)
+    hop(2, 1, 0)
     line(2)
+    ring(1)
     hop(0, 2, 1)
+    hop(1, 1, 1)
+    pair(2)
     hop(0, 4, 0)
-    ring(1)
-    pair(1)
-    hop(1, 1, 0)
-    own(2)
+    hop(1, 3, 0)
+    hop(2, 2, 0)
+    line(3)
+    ring(2)
     hop(0, 3, 1)
-    line(3)
-    hop(1, 2, 0)
+    hop(1, 2, 1)
+    hop(2, 1, 1)
+    hop(1, 4, 0)
+    hop(2, 3, 0)
+    ring(3)
     hop(0, 4, 1)
-    ring(2)
-    hop(1, 1, 1)
+    hop(1, 3, 1)
+    hop(2, 2, 1)
+    hop(2, 4, 0)
     fill(0)
     first(0)
     first(1)
-    hop(1, 3, 0)
     first(2)
-    hop(1, 2, 1)
     first(3)
     keep(0).start()
-    pair(2)
-    hop(1, 4, 0)
-    hop(2, 1, 0)
-    ring(3)
-    hop(1, 3, 1)
-    hop(2, 2, 0)
     hop(1, 4, 1)
-    hop(2, 1, 1)
+    hop(2, 3, 1)
     fill(1)
-    carried(0, 2)
-    hop(2, 3, 0)
-    carried(2, 4)
-    hop(2, 2, 1)
-    hop(2, 4, 0)
+    carried(0, 4)
     ringlast()
     ready(load_t)
     update_first(0, 2)
-    hop(2, 3, 1)
+    hop(2, 4, 1)
     update_first(2, 4)
-    hop(2, 4, 1)
     fill(2)
-    for i in range(4):
-        second(i)
+    second(0)
+    second(1)
+    second(2)
+    second(3)
     keep(1).start()
     update_second()
 
@@ -326,7 +327,7 @@
             jax.ShapeDtypeStruct((2, 32, 1024), BF),
             jax.ShapeDtypeStruct((1024, 1024), BF),
         ),
-        in_specs=[anywhere] * 5,
+        in_specs=[pl.BlockSpec(memory_space=pltpu.HBM)] * 5,
         out_specs=(anywhere, anywhere),
         scratch_shapes=[
             pltpu.VMEM((3, 1024, 1024), BF),
@@ -346,7 +347,7 @@
             dma((4,)),
         ],
         compiler_params=pltpu.CompilerParams(
-            collective_id=0, has_side_effects=True, vmem_limit_bytes=60 * 1024 * 1024
+            collective_id=0, has_side_effects=True, vmem_limit_bytes=50 * 1024 * 1024
         ),
         name="substitute",
     )(rhs_top, diag_inverse, panel_coupling, trailing_factor, rhs_trailing)

time: 93.6 us -> 87.5 us (0.935)
  Pallas kernels: 88.2 us -> 81 us
    pallas_call x1, Pallas kernels: 88.2 us -> 81 us  [shards(): pl.pallas_call(kernel, out_shape=(jax.ShapeDtypeStruct((2, 32, 1024), BF)...]
    unnamed x2 -> x10, local copies, waits for them, and re-layouts: 4.65 us -> 5.57 us
where the time goes in v3:
time: 87.5 us; the launch traced here: 87.2 us
  Pallas kernels  81 us (93%)
  local copies, waits for them, and re-layouts  5.57 us (6%)
    pallas_call x1, Pallas kernels, shards(): pl.pallas_call(kernel, out_shape=(jax.ShapeDtypeStruct((2, 32, 1024), BF)...  81 us
    unnamed x10, local copies, waits for them, and re-layouts  5.57 us

profile of v3, /device:TPU:1, one launch (start us, length us, event | category | flops | bytes accessed | tf_op | source)
XLA Modules:
  0.0 87.2 jit_solution(8992199834609258155)
XLA Ops:
  0.6 0.0 copy-start
  0.6 0.9 %copy-done = bf16[1024,128]{1,0:T(8,128)(2,1)S(1)} copy-done((bf16[1024,128]{1,0:T(8,128)(2,1)S(1)}, bf16[1024,128]{1,0:T(8,128)(2,1)}, u32[]{:S(2)}) %copy-start) | copy-done | bytes 262168
  1.6 0.0 copy-start.1
  1.6 0.9 %copy-done.1 = bf16[2,32,1024]{2,1,0:T(8,128)(2,1)S(1)} copy-done((bf16[2,32,1024]{2,1,0:T(8,128)(2,1)S(1)}, bf16[2,32,1024]{2,1,0:T(8,128)(2,1)}, u32[]{:S(2)}) %copy-start.1) | copy-done | bytes 131096
  2.5 0.0 copy-start.2
  2.5 0.9 %copy-done.2 = bf16[2,32,1024]{2,1,0:T(8,128)(2,1)S(1)} copy-done((bf16[2,32,1024]{2,1,0:T(8,128)(2,1)S(1)}, bf16[2,32,1024]{2,1,0:T(8,128)(2,1)}, u32[]{:S(2)}) %copy-start.2) | copy-done | bytes 131096
  3.4 0.0 copy-start.3
  3.4 0.8 copy-done.3
  4.2 81.0 %substitute.1 = (bf16[2,32,1024]{2,1,0:T(8,128)(2,1)S(1)}, bf16[1024,1024]{1,0:T(8,128)(2,1)S(1)}) custom-call(bf16[2,32,1024]{2,1,0:T(8,128)(2,1)S(1)} %copy-done.1, bf16[2,32,1024]{2,1,0:T(8,128)(2,1)S(1)} %copy-done.2, bf16[32,1024]{1,0:T(8,128)(2,1)S(1)} %copy-done.3, bf16[1024,128]{1,0:T(8,128)(2,1)S(1)} %copy-done, bf16[1024,1024]{1,0:T(8,128)(2,1)} %trail_ref.1), custom_call_target="tpu_custom_call" | custom-call | tf_op jit(solution)/shard_map/substitute/pallas_call | solution.py:324
  85.2 0.7 copy.9
  85.9 1.3 %copy.10 = bf16[1024,1024]{1,0:T(8,128)(2,1)} copy(bf16[1024,1024]{1,0:T(8,128)(2,1)S(1)} %get-tuple-element.5) | data formatting | bytes 4194304
Async XLA Ops:
  0.6 1.0 %copy-start = (bf16[1024,128]{1,0:T(8,128)(2,1)S(1)}, bf16[1024,128]{1,0:T(8,128)(2,1)}, u32[]{:S(2)}) copy-start(bf16[1024,128]{1,0:T(8,128)(2,1)} %fac_ref.1) | copy-start | bytes 786436
  1.6 0.9 %copy-start.1 = (bf16[2,32,1024]{2,1,0:T(8,128)(2,1)S(1)}, bf16[2,32,1024]{2,1,0:T(8,128)(2,1)}, u32[]{:S(2)}) copy-start(bf16[2,32,1024]{2,1,0:T(8,128)(2,1)} %rhs_ref.1) | copy-start | bytes 393220
  2.5 0.9 %copy-start.2 = (bf16[2,32,1024]{2,1,0:T(8,128)(2,1)S(1)}, bf16[2,32,1024]{2,1,0:T(8,128)(2,1)}, u32[]{:S(2)}) copy-start(bf16[2,32,1024]{2,1,0:T(8,128)(2,1)} %diag_ref.1) | copy-start | bytes 393220
  3.4 0.8 copy-start.3

commit v4 on v3

--- a/solution.py
+++ b/solution.py
@@ -280,13 +280,13 @@
     first(2)
     first(3)
     keep(0).start()
-    hop(1, 4, 1)
     hop(2, 3, 1)
-    fill(1)
-    carried(0, 4)
     ringlast()
     ready(load_t)
     update_first(0, 2)
+    hop(1, 4, 1)
+    fill(1)
+    carried(0, 4)
     hop(2, 4, 1)
     update_first(2, 4)
     fill(2)

time: 87.5 us -> 88.9 us (1.016)
  Pallas kernels: 81 us -> 82.4 us
    pallas_call x1, Pallas kernels: 81 us -> 82.4 us  [shards(): pl.pallas_call(kernel, out_shape=(jax.ShapeDtypeStruct((2, 32, 1024), BF)...]
where the time goes in v4:
time: 88.9 us; the launch traced here: 88.7 us
  Pallas kernels  82.4 us (93%)
  local copies, waits for them, and re-layouts  5.57 us (6%)
    pallas_call x1, Pallas kernels, shards(): pl.pallas_call(kernel, out_shape=(jax.ShapeDtypeStruct((2, 32, 1024), BF)...  82.4 us
    unnamed x10, local copies, waits for them, and re-layouts  5.57 us

profile of v4, /device:TPU:1, one launch (start us, length us, event | category | flops | bytes accessed | tf_op | source)
XLA Modules:
  0.0 88.7 jit_solution(11224932832367138272)
XLA Ops:
  0.6 0.0 copy-start
  0.6 0.9 %copy-done = bf16[1024,128]{1,0:T(8,128)(2,1)S(1)} copy-done((bf16[1024,128]{1,0:T(8,128)(2,1)S(1)}, bf16[1024,128]{1,0:T(8,128)(2,1)}, u32[]{:S(2)}) %copy-start) | copy-done | bytes 262168
  1.6 0.0 copy-start.1
  1.6 0.9 %copy-done.1 = bf16[2,32,1024]{2,1,0:T(8,128)(2,1)S(1)} copy-done((bf16[2,32,1024]{2,1,0:T(8,128)(2,1)S(1)}, bf16[2,32,1024]{2,1,0:T(8,128)(2,1)}, u32[]{:S(2)}) %copy-start.1) | copy-done | bytes 131096
  2.5 0.0 copy-start.2
  2.5 0.9 %copy-done.2 = bf16[2,32,1024]{2,1,0:T(8,128)(2,1)S(1)} copy-done((bf16[2,32,1024]{2,1,0:T(8,128)(2,1)S(1)}, bf16[2,32,1024]{2,1,0:T(8,128)(2,1)}, u32[]{:S(2)}) %copy-start.2) | copy-done | bytes 131096
  3.4 0.0 copy-start.3
  3.4 0.8 copy-done.3
  4.2 82.4 %substitute.1 = (bf16[2,32,1024]{2,1,0:T(8,128)(2,1)S(1)}, bf16[1024,1024]{1,0:T(8,128)(2,1)S(1)}) custom-call(bf16[2,32,1024]{2,1,0:T(8,128)(2,1)S(1)} %copy-done.1, bf16[2,32,1024]{2,1,0:T(8,128)(2,1)S(1)} %copy-done.2, bf16[32,1024]{1,0:T(8,128)(2,1)S(1)} %copy-done.3, bf16[1024,128]{1,0:T(8,128)(2,1)S(1)} %copy-done, bf16[1024,1024]{1,0:T(8,128)(2,1)} %trail_ref.1), custom_call_target="tpu_custom_call" | custom-call | tf_op jit(solution)/shard_map/substitute/pallas_call | solution.py:324
  86.7 0.7 copy.9
  87.3 1.3 %copy.10 = bf16[1024,1024]{1,0:T(8,128)(2,1)} copy(bf16[1024,1024]{1,0:T(8,128)(2,1)S(1)} %get-tuple-element.5) | data formatting | bytes 4194304
Async XLA Ops:
  0.6 1.0 %copy-start = (bf16[1024,128]{1,0:T(8,128)(2,1)S(1)}, bf16[1024,128]{1,0:T(8,128)(2,1)}, u32[]{:S(2)}) copy-start(bf16[1024,128]{1,0:T(8,128)(2,1)} %fac_ref.1) | copy-start | bytes 786436
  1.6 0.9 %copy-start.1 = (bf16[2,32,1024]{2,1,0:T(8,128)(2,1)S(1)}, bf16[2,32,1024]{2,1,0:T(8,128)(2,1)}, u32[]{:S(2)}) copy-start(bf16[2,32,1024]{2,1,0:T(8,128)(2,1)} %rhs_ref.1) | copy-start | bytes 393220
  2.5 0.9 %copy-start.2 = (bf16[2,32,1024]{2,1,0:T(8,128)(2,1)S(1)}, bf16[2,32,1024]{2,1,0:T(8,128)(2,1)}, u32[]{:S(2)}) copy-start(bf16[2,32,1024]{2,1,0:T(8,128)(2,1)} %diag_ref.1) | copy-start | bytes 393220
  3.4 0.8 copy-start.3
